TPU v7x, 1024 devices: a whole 8x8x8 slice. The times are simulated.
1024 devices in a mesh: replica: 128 (over z, y, core), tensor: 8 (over x).
Axes of the slice: x: 8, y: 8, z: 8, core: 2. Of those that a mesh axis runs over, the one named last changes fastest.
Arguments:
- base_stream: bfloat16 [512, 8192], P('tensor', 'replica'), may hold values from -6 to 6
- out_weight: bfloat16 [64, 128, 8192], P('tensor', 'replica'), may hold values from -0.5 to 0.5
- queries: bfloat16 [4, 512, 64, 128], P(None, 'replica', 'tensor'), may hold values from -5 to 5
- cache_keys: bfloat16 [512, 8, 1536, 128], P('replica', 'tensor'), may hold values from -5 to 5
- cache_values: bfloat16 [512, 8, 1536, 128], P('replica', 'tensor'), may hold values from -6 to 6
- new_keys: bfloat16 [4, 512, 8, 128], P(None, 'replica', 'tensor'), may hold values from -5 to 5
- new_values: bfloat16 [4, 512, 8, 128], P(None, 'replica', 'tensor'), may hold values from -6 to 6
- lengths: int32 [512], P('replica'), may hold values from 384 to 1536
- finished: int32 [512], replicated, may hold values 0 or 1
- owners: int32 [512, 1], replicated, may hold values from 0 to 127; in each aligned block of 512 rows (0 to 511, 512 to 1023, ...) at most 8 rows name the same one
Outputs:
- updates: bfloat16 [4, 512, 8192], P(None, 'tensor', 'replica')
- trainer_rows: bfloat16 [128, 8, 8192], P('replica', 'tensor')
Inputs may be any that keep to these rules, and one draw needn't show every extreme that they name: `owners`: no owner is named by more than 8 rows, and one owner is named by exactly 8.
All inputs are finite; a program needn't handle non-finite values.
Results may differ from a plain program's by a relative error of at most 0.013.
Values may be sent and summed in bfloat16 or wider, within the bound.
A program may use at most 64 MiB of HBM per device.

v0:
```python
import math

import jax
import jax.numpy as jnp
from jax import lax
from jax.sharding import Mesh
from jax.sharding import PartitionSpec as P

SLOT_DEV = 1
REPLICA = ("replica_0", "replica_1", "replica_2")


def gathered_total(shard, axis):
    pieces = lax.all_gather(shard, axis).astype(jnp.float32)
    return pieces.sum(axis=0)


def in_blocks(shard, dim, length):
    before, after = (shard.shape[:dim], shard.shape[dim + 1 :])
    return jnp.moveaxis(shard.reshape(*before, length, -1, *after), dim, 0)


def laid_out(pieces, dim):
    dims = list(pieces.shape[1:])
    dims[dim] *= pieces.shape[0]
    return jnp.moveaxis(pieces, 0, dim).reshape(dims)


def turned_blocks(pieces, axes, turns):
    inside = pieces.shape[1:]
    result = pieces.reshape(*(lax.axis_size(a) for a in axes), *inside)
    for k in turns:
        result = lax.all_to_all(result, axes[k], k, k, tiled=True)
    return result.reshape(-1, *inside)


def exchange_by_chip(shard, groups, turns, split_dim, concat_dim):
    length = lax.axis_size(groups[0]) * lax.axis_size(groups[1])
    pieces = in_blocks(shard, split_dim, length)
    return laid_out(turned_blocks(pieces, groups, turns), concat_dim)


def sent_to_all(shard, axis):
    length = lax.axis_size(axis)
    return lax.all_to_all(
        jnp.broadcast_to(shard[None], (length, *shard.shape)), axis, 0, 0, tiled=True
    )


def collect(shard, axis, dim):
    pieces = sent_to_all(shard, axis)
    return laid_out(pieces, dim)


def attend(queries, cache_keys, cache_values, new_keys, new_values, lengths):
    steps_count, row_count, heads_here, head_size = queries.shape
    kv_here = cache_keys.shape[1]
    positions_count = cache_keys.shape[2]
    group_size = heads_here // kv_here
    score_scale = 1.0 / math.sqrt(head_size)
    grouped = queries.reshape(steps_count, row_count, kv_here, group_size, head_size)
    cache_scores = (
        jnp.einsum("tbgqd,bgcd->tbgqc", grouped, cache_keys, preferred_element_type=jnp.float32)
        * score_scale
    )
    positions = lax.broadcasted_iota(jnp.int32, (1, row_count, 1, 1, positions_count), 4)
    is_valid = positions < lengths[None, :, None, None, None]
    cache_scores = jnp.where(is_valid, cache_scores, jnp.float32(-1e30))
    fresh_scores = (
        jnp.einsum("tbgqd,ubgd->tbgqu", grouped, new_keys, preferred_element_type=jnp.float32)
        * score_scale
    )
    step_now = lax.broadcasted_iota(jnp.int32, (steps_count, 1, 1, 1, steps_count), 0)
    step_then = lax.broadcasted_iota(jnp.int32, (steps_count, 1, 1, 1, steps_count), 4)
    fresh_scores = jnp.where(step_then <= step_now, fresh_scores, jnp.float32(-1e30))
    highest = jnp.maximum(
        jnp.max(cache_scores, axis=-1, keepdims=True), jnp.max(fresh_scores, axis=-1, keepdims=True)
    )
    cache_weights = jnp.exp(cache_scores - highest)
    fresh_weights = jnp.exp(fresh_scores - highest)
    totals = jnp.sum(cache_weights, axis=-1, keepdims=True) + jnp.sum(
        fresh_weights, axis=-1, keepdims=True
    )
    cache_probs = (cache_weights / totals).astype(jnp.bfloat16)
    fresh_probs = (fresh_weights / totals).astype(jnp.bfloat16)
    mixed = jnp.einsum(
        "tbgqc,bgcd->tbgqd", cache_probs, cache_values, preferred_element_type=jnp.float32
    )
    mixed = mixed + jnp.einsum(
        "tbgqu,ubgd->tbgqd", fresh_probs, new_values, preferred_element_type=jnp.float32
    )
    return mixed.reshape(steps_count, row_count, heads_here * head_size).astype(jnp.bfloat16)


def reduce_heads(partial_value):
    rounded = partial_value.astype(jnp.bfloat16)
    totals = gathered_total(rounded, "tensor").astype(jnp.float32)
    share = totals.shape[1] // lax.axis_size("tensor")
    return lax.dynamic_slice_in_dim(totals, lax.axis_index("tensor") * share, share, 1)


def shards(
    base_stream,
    out_weight,
    queries,
    cache_keys,
    cache_values,
    new_keys,
    new_values,
    lengths,
    finished,
    owners,
):
    heads_here = out_weight.shape[0]
    regrouped = exchange_by_chip(
        out_weight, (("replica_0", "replica_1"), "replica_2"), (1, 0), 2, 1
    )
    weight_local = regrouped.reshape(heads_here * regrouped.shape[1], regrouped.shape[2])
    attended = attend(queries, cache_keys, cache_values, new_keys, new_values, lengths)
    partial_value = jnp.einsum(
        "tbf,fc->tbc",
        lax.all_gather(attended, REPLICA, axis=1, tiled=True),
        weight_local,
        preferred_element_type=jnp.float32,
    )
    summed = reduce_heads(partial_value)
    updates = summed.astype(jnp.bfloat16)
    stream = base_stream.astype(jnp.float32) + jnp.sum(updates.astype(jnp.float32), axis=0)
    stream_rounded = stream.astype(jnp.bfloat16)
    all_streams = collect(stream_rounded, "tensor", 0)
    owner_count = lax.axis_size(REPLICA)
    owner_ids = lax.broadcasted_iota(jnp.int32, (1, owner_count), 1)
    onehot = (owners == owner_ids).astype(jnp.int32)
    before = jnp.cumsum(onehot, axis=0) - onehot
    slot_rank = jnp.sum(before * onehot, axis=1)
    first_slot = lax.axis_index("tensor") * SLOT_DEV
    slot_ids = first_slot + lax.broadcasted_iota(jnp.int32, (1, 1, SLOT_DEV), 2)
    chosen = (
        onehot[:, :, None]
        * (slot_rank[:, None, None] == slot_ids).astype(jnp.int32)
        * finished[:, None, None]
    )
    selector = chosen.astype(jnp.bfloat16)
    outgoing = jnp.einsum(
        "jos,jc->osc", selector, all_streams, preferred_element_type=jnp.float32
    ).astype(jnp.bfloat16)
    trainer_rows = lax.all_to_all(outgoing, REPLICA, split_axis=0, concat_axis=2, tiled=True)
    return (updates, trainer_rows)


def solution(mesh):
    torus = Mesh(
        mesh.devices.reshape(8, 8, 2, mesh.shape["tensor"]),
        ("replica_0", "replica_1", "replica_2", "tensor"),
    )
    placed = (
        P("tensor", REPLICA),
        P("tensor", REPLICA, None),
        P(None, REPLICA, "tensor", None),
        P(REPLICA, "tensor", None, None),
        P(REPLICA, "tensor", None, None),
        P(None, REPLICA, "tensor", None),
        P(None, REPLICA, "tensor", None),
        P(REPLICA),
        P(),
        P(),
    )
    return jax.shard_map(
        shards,
        mesh=torus,
        in_specs=placed,
        out_specs=(P(None, "tensor", REPLICA), P(REPLICA, "tensor", None)),
        check_vma=False,
    )
```

profile of v0, /device:TPU:1, one launch (start us, length us, event | category | flops | bytes accessed | tf_op | source)
XLA Modules:
  0.0 215.9 jit_solution(14145592589798596992)
XLA Ops:
  7.2 0.0 copy-start
  7.2 0.0 copy-start.5
  7.2 0.0 copy-start.4
  7.2 0.0 all-gather.4.cloned.1.call-start
  7.3 0.9 iota_compare_fusion.3
  8.1 1.0 fusion.45
  9.2 0.0 copy-done
  9.2 1.5 fusion.44
  10.7 0.3 fusion.23
  11.0 0.0 copy-done.5
  11.0 0.2 fusion.38
  11.2 0.0 copy-done.4
  11.2 0.0 copy-start.1
  11.2 0.4 fusion.17
  11.7 0.6 convert_element_type.76
  12.3 0.0 all-gather.4.cloned.1.call-update
  12.3 0.0 all-gather.6.cloned.1.call-start
  12.4 0.0 copy-done.1
  12.4 0.2 reshape.190
  12.6 0.2 copy.83
  12.8 0.2 reshape.204
  13.1 17.6 %all_to_all.27 = bf16[2,2,16384]{2,1,0:T(2,128)(2,1)S(1)} all-to-all(bf16[2,2,16384]{2,1,0:T(2,128)(2,1)S(1)} %reshape.204), channel_id=1, replica_groups=mesh['replica_0'=8,'replica_1'=8,'replica_2'=2,'tensor'=8] {'replica_2'}, dimensions={0} | all-to-all | bytes 262144 | tf_op jit(solution)/shard_map/all_to_all | solution.py:33
  30.7 0.2 reshape.205
  30.9 0.2 reshape.206
  31.1 21.8 %all_to_all.28 = bf16[64,2,512]{2,1,0:T(2,128)(2,1)S(1)} all-to-all(bf16[64,2,512]{2,1,0:T(2,128)(2,1)S(1)} %reshape.206), channel_id=1, replica_groups=mesh['replica_0'=8,'replica_1'=8,'replica_2'=2,'tensor'=8] {'replica_0',..., dimensions={0} | all-to-all | bytes 262144 | tf_op jit(solution)/shard_map/all_to_all | solution.py:33
  53.0 0.2 reshape.207
  53.2 0.2 copy.47
  53.4 0.1 reshape.201
  53.5 0.0 copy-start.2
  53.5 0.0 copy-start.3
  53.5 63.9 %all-gather.4.cloned.1.call-done = bf16[4,512,1024]{2,0,1:T(4,128)(2,1)} async-done(((bf16[4,4,1024]{2,0,1:T(4,128)(2,1)}), bf16[4,512,1024]{2,0,1:T(4,128)(2,1)}) %all-gather.4.cloned.1.call-update) | async-done | bytes 4194320 | tf_op jit(solution)/shard_map/all_gather | solution.py:122
  117.4 5.4 %fusion.8 = bf16[4,512,64]{1,2,0:T(8,128)(2,1)} fusion(bf16[1024,64,1]{0,1,2:T(8,128)(2,1)S(1)} %reshape.201, bf16[4,512,1024]{2,0,1:T(4,128)(2,1)} %all-gather.4.cloned.1.call-done), kind=kOutput, calls=%fused_computation.10 | convolution fusion | flops 268566528 | bytes 4587520 | tf_op jit(solution)/shard_map/tbf,fc->tbc/dot_general | solution.py:120
  122.7 0.0 all-gather.6.cloned.1.call-update
  122.8 0.0 copy-done.2
  122.8 0.1 copy.51
  122.9 0.0 copy-done.3
  122.9 0.1 copy.49
  123.0 0.2 fusion.28
  123.3 0.0 copy-start.6
  123.3 0.2 fusion.27
  123.6 36.9 %all-gather.6.cloned.1.call-done = bf16[32,512,64]{1,2,0:T(8,128)(2,1)} async-done(((bf16[4,512,64]{1,2,0:T(8,128)(2,1)}), bf16[32,512,64]{1,2,0:T(8,128)(2,1)}) %all-gather.6.cloned.1.call-update) | async-done | bytes 2097168 | tf_op jit(solution)/shard_map/all_gather | solution.py:14
  160.5 1.9 convert_reduce_fusion
  162.4 0.1 convert_reduce_fusion.1
  162.5 0.1 copy.52
  162.6 0.8 reshape.208
  163.4 3.7 %all-to-all-start.2 = ((bf16[8,2,2048]{2,1,0:T(2,128)(2,1)}), bf16[8,2,2048]{2,1,0:T(2,128)(2,1)S(1)}, u32[]{:S(2)}, u32[]{:S(2)}) async-start(bf16[8,2,2048]{2,1,0:T(2,128)(2,1)} %reshape.208), calls=%async_computation.2 | async-start | bytes 131072 | tf_op jit(solution)/shard_map/all_to_all | solution.py:45
  167.2 7.2 %all-to-all-done.2 = bf16[8,2,2048]{2,1,0:T(2,128)(2,1)S(1)} async-done(((bf16[8,2,2048]{2,1,0:T(2,128)(2,1)}), bf16[8,2,2048]{2,1,0:T(2,128)(2,1)S(1)}, u32[]{:S(2)}, u32[]{:S(2)}) %all-to-all-start.2) | async-done | bytes 65568 | tf_op jit(solution)/shard_map/all_to_all | solution.py:45
  174.4 0.1 reshape.209
  174.5 0.0 copy-done.6
  174.6 0.4 fusion.21
  175.0 0.8 copy.53
  175.7 21.0 %all-to-all-start.3 = ((bf16[128,1,64]{2,1,0:T(2,128)(2,1)}), bf16[128,1,64]{2,1,0:T(2,128)(2,1)S(1)}, u32[]{:S(2)}, u32[]{:S(2)}) async-start(bf16[128,1,64]{2,1,0:T(2,128)(2,1)} %copy.53), calls=%async_computation.3 | async-start | bytes 131072 | tf_op jit(solution)/shard_map/all_to_all | solution.py:147
  196.7 0.7 copy.54
  197.5 10.7 %all-to-all-done.3 = bf16[128,1,64]{2,1,0:T(2,128)(2,1)S(1)} async-done(((bf16[128,1,64]{2,1,0:T(2,128)(2,1)}), bf16[128,1,64]{2,1,0:T(2,128)(2,1)S(1)}, u32[]{:S(2)}, u32[]{:S(2)}) %all-to-all-start.3) | async-done | bytes 16416 | tf_op jit(solution)/shard_map/all_to_all | solution.py:147
  208.2 0.2 reduce.4
  208.4 0.7 all_to_all.22
  (14 shorter events, 0.2 us)
Async XLA Ops:
  7.2 2.0 copy-start
  7.2 3.8 %copy-start.5 = (bf16[4,4,1,128]{3,1,2,0:T(4,128)(2,1)S(1)}, bf16[4,4,1,128]{3,1,2,0:T(4,128)(2,1)}, u32[]{:S(2)}) copy-start(bf16[4,4,1,128]{3,1,2,0:T(4,128)(2,1)} %param.16) | copy-start | bytes 12292
  7.2 4.0 %copy-start.4 = (bf16[4,1,1536,128]{3,2,1,0:T(8,128)(2,1)S(1)}, bf16[4,1,1536,128]{3,2,1,0:T(8,128)(2,1)}, u32[]{:S(2)}) copy-start(bf16[4,1,1536,128]{3,2,1,0:T(8,128)(2,1)} %param.14) | copy-start | bytes 4718596
  7.2 110.2 %all-gather.4.cloned.1.call-start = ((), (), s32[]{:S(2)}) async-start(), calls=%async_computation.4 | async-start | bytes 4227072 | tf_op jit(solution)/shard_map/all_gather | solution.py:122
  11.2 1.1 copy-start.1
  12.3 148.2 %all-gather.6.cloned.1.call-start = ((), (), s32[]{:S(2)}) async-start(), calls=%async_computation.5 | async-start | bytes 2359296 | tf_op jit(solution)/shard_map/all_gather | solution.py:14
  53.5 69.3 %copy-start.2 = (bf16[64,64]{1,0:T(8,128)(2,1)S(1)}, bf16[64,64]{1,0:T(8,128)(2,1)}, u32[]{:S(2)}) copy-start(bf16[64,64]{1,0:T(8,128)(2,1)} %param.10) | copy-start | bytes 24580
  53.5 69.4 %copy-start.3 = (s32[512,1]{0,1:T(1,128)S(1)}, s32[512,1]{0,1:T(1,128)}, u32[]{:S(2)}) copy-start(s32[512,1]{0,1:T(1,128)} %param.19) | copy-start | bytes 6148
  123.3 51.3 %copy-start.6 = (s32[512]{0:T(512)S(1)}, s32[512]{0:T(512)}, u32[]{:S(2)}) copy-start(s32[512]{0:T(512)} %param.18) | copy-start | bytes 6148
  163.4 11.0 %all-to-all-start.2 = ((bf16[8,2,2048]{2,1,0:T(2,128)(2,1)}), bf16[8,2,2048]{2,1,0:T(2,128)(2,1)S(1)}, u32[]{:S(2)}, u32[]{:S(2)}) async-start(bf16[8,2,2048]{2,1,0:T(2,128)(2,1)} %reshape.208), calls=%async_computation.2 | async-start | bytes 131072 | tf_op jit(solution)/shard_map/all_to_all | solution.py:45
  175.7 32.5 %all-to-all-start.3 = ((bf16[128,1,64]{2,1,0:T(2,128)(2,1)}), bf16[128,1,64]{2,1,0:T(2,128)(2,1)S(1)}, u32[]{:S(2)}, u32[]{:S(2)}) async-start(bf16[128,1,64]{2,1,0:T(2,128)(2,1)} %copy.53), calls=%async_computation.3 | async-start | bytes 131072 | tf_op jit(solution)/shard_map/all_to_all | solution.py:147
Sparse Core Ops, SparseCore 0:
  12.9 104.4 all-gather.3
  122.9 37.5 all-gather.5
where the time goes:
time: 216 us
  waiting for transfers between devices  119 us (55%)
  blocking collectives  39.4 us (18%)
  starting transfers between devices  24.8 us (11%)
  between operations  14.3 us (7%)
  matrix products  8.95 us (4%)
  local copies, waits for them, and re-layouts  5.74 us (3%)
  other arithmetic  3.91 us (2%)
    all_gather x1, waiting for transfers between devices, shards(): lax.all_gather(attended, REPLICA, axis=1, tiled=True)  63.9 us
    all_to_all x2, blocking collectives, turned_blocks(): result = lax.all_to_all(result, axes[k], k, k, tiled=True)  39.4 us
    all_gather x1, waiting for transfers between devices, gathered_total(): pieces = lax.all_gather(shard, axis).astype(jnp.float32)  36.9 us
    all_to_all x1, starting transfers between devices, shards(): lax.all_to_all(outgoing, REPLICA, split_axis=0, concat_axis=2, tiled=True)  21 us
    all_to_all x1, waiting for transfers between devices, shards(): lax.all_to_all(outgoing, REPLICA, split_axis=0, concat_axis=2, tiled=True)  10.7 us
    all_to_all x1, waiting for transfers between devices, sent_to_all(): lax.all_to_all(jnp.broadcast_to(shard[None], (length, *shard.shape)), axi...  7.22 us
    dot_general x1, matrix products, shards(): jnp.einsum('tbf,fc->tbc', lax.all_gather(attended, REPLICA, axis=1, tiled...  5.37 us
  transfers between devices with their start and end apart: 4, of which 4 were waited for; matrix products, arithmetic and copies ran while one was open for 1% of the time, Pallas kernels for 0%

commit v1 on v0

v1 whole, which is shorter than its diff:
```python
import functools
import math

import jax
import jax.numpy as jnp
from jax import lax
from jax.experimental import pallas as pl
from jax.experimental.pallas import tpu as pltpu
from jax.sharding import Mesh
from jax.sharding import PartitionSpec as P

ZA, YA, CA, XA = "replica_0", "replica_1", "replica_2", "tensor"
REPLICA = (ZA, YA, CA)
MESH = pl.DeviceIdType.MESH
F32, BF16, I32 = jnp.float32, jnp.bfloat16, jnp.int32
N = 8
CTX = 1536
PAD = 128
FULL = CTX + PAD
ROWS = 512


def dot(a, b):
    return jnp.dot(a, b, preferred_element_type=F32)


def iota(shape, dim):
    return lax.broadcasted_iota(I32, shape, dim)


def offset_of(j):
    return (j + 1) // 2 * (2 * (j % 2) - 1)


def mirror(j):
    if j == 0 or j == N - 1:
        return j
    return j + 1 if j % 2 else j - 1


def kernel(
    len_ref, q_hbm, k_hbm, v_hbm, nk_hbm, nv_hbm, w_hbm, base_hbm, own_hbm, fin_hbm,
    upd_hbm, tr_hbm,
    q_v, k_v, v_v, nk_v, nv_v, base_v, own_v, fin_v,
    s1, wbuf, wf, w4, att, g0, g1, cs, cr, sp, sg, sgu, oh, o1, r1, tf, t2, r2, uout, trout,
    in_sem, kv_sem, out_sem,
    w_send, w1_recv, w2_recv, w3_recv,
    p_send, p_recv, ring_send, ring_recv,
    c_send, c_recv, s_send, s_recv, z_send, z_recv, y_send, y_recv,
):
    z, y, c, x = (lax.axis_index(a) for a in (ZA, YA, CA, XA))
    other = 1 - c

    def rot(i, d):
        return lax.rem(i + d + N, N)

    def remote(src, dst, ssem, rsem, **to):
        pltpu.make_async_remote_copy(
            src_ref=src, dst_ref=dst, send_sem=ssem, recv_sem=rsem,
            device_id={{"z": ZA, "y": YA, "c": CA, "x": XA}[k]: v for k, v in to.items()},
            device_id_type=MESH,
        ).start()

    def arrived(ref, sem):
        pltpu.make_async_copy(ref, ref, sem).wait()

    small = [
        (q_hbm, q_v), (nk_hbm, nk_v), (nv_hbm, nv_v), (base_hbm, base_v), (own_hbm, own_v), (fin_hbm, fin_v),
    ]
    loads = [pltpu.make_async_copy(a, b, in_sem.at[i]) for i, (a, b) in enumerate(small)]
    k_loads = [pltpu.make_async_copy(k_hbm.at[b], k_v.at[b, pl.ds(0, CTX)], kv_sem.at[0, b]) for b in range(4)]
    v_loads = [pltpu.make_async_copy(v_hbm.at[b], v_v.at[b, pl.ds(0, CTX)], kv_sem.at[1, b]) for b in range(4)]
    for load in loads[:3]:
        load.start()
    for b in range(4):
        k_loads[b].start()
        v_loads[b].start()
    for load in loads[3:]:
        load.start()

    barrier = pltpu.get_barrier_semaphore()

    def greet(**to):
        pl.semaphore_signal(
            barrier, inc=1, device_id={{"z": ZA, "y": YA, "c": CA, "x": XA}[k]: v for k, v in to.items()},
            device_id_type=MESH,
        )

    greet(c=other)

    def greet_step(d, carry):
        greet(z=rot(z, d))
        greet(y=rot(y, d), c=0)
        greet(y=rot(y, d), c=1)
        greet(x=rot(x, d), c=0)
        greet(x=rot(x, d), c=1)
        return carry

    lax.fori_loop(1, N, greet_step, 0)

    for load in loads[:3]:
        load.wait()
    nk, nv = nk_v[...], nv_v[...]
    for b in range(4):
        pick = (iota((PAD, 16), 1) == iota((PAD, 16), 0) * 4 + b).astype(F32).astype(BF16)
        k_v[b, CTX:FULL, :] = dot(pick, nk).astype(BF16)
        v_v[b, CTX:FULL, :] = dot(pick, nv).astype(BF16)

    scale = 1.0 / math.sqrt(128.0)

    def attend(b):
        q = q_v[:, b].astype(F32).reshape(32, 128).astype(BF16)
        k_loads[b].wait()
        scores = lax.dot_general(q, k_v[b], (((1,), (1,)), ((), ())), preferred_element_type=F32) * scale
        col = iota((32, FULL), 1)
        step = iota((32, FULL), 0) // 8
        keep = (col < len_ref[b]) | ((col >= CTX) & (col - CTX <= step))
        scores = jnp.where(keep, scores, F32(-1e30))
        high = jnp.max(scores, axis=-1, keepdims=True)
        weight = jnp.exp(scores - high)
        total = jnp.sum(weight, axis=-1, keepdims=True)
        probs = (weight / total).astype(BF16)
        v_loads[b].wait()
        mixed = dot(probs, v_v[b])
        for t in range(4):
            att[pl.ds((t * 4 + b) * 8, 8), :] = mixed[t * 8 : t * 8 + 8]

    attend(0)
    attend(1)
    pl.semaphore_wait(barrier, 5 * (N - 1) + 1)

    own_w = pltpu.make_async_copy(w_hbm.at[:, pl.ds(pl.multiple_of(z * 1024, 1024), 1024)], s1.at[z], in_sem.at[6])
    own_w.start()

    def w1_step(d, carry):
        zt = rot(z, d)
        remote(w_hbm.at[:, pl.ds(pl.multiple_of(zt * 1024, 1024), 1024)], s1.at[z], w_send.at[0], w1_recv.at[d], z=zt)
        return carry

    lax.fori_loop(1, N, w1_step, 0)
    attend(2)
    attend(3)
    for h in range(8):
        part = att[pl.ds(h, 16, stride=8), :].astype(BF16)
        (g0 if h < 4 else g1)[z, y, :, (h % 4) * 128 : (h % 4) * 128 + 128] = part

    for j in range(1, N):
        o = offset_of(j)
        remote(g0.at[z, y], g0.at[z, y], p_send.at[0], p_recv.at[0, mirror(j)], y=rot(y, o))
        remote(g1.at[z, y], g1.at[z, y], p_send.at[1], p_recv.at[1, mirror(j)], z=rot(z, o))

    def unit(stream, s, j):
        o = offset_of(j)
        if stream == 0:
            return g0.at[rot(z, -s), rot(y, o)]
        if stream == 1:
            return g0.at[rot(z, s), rot(y, o)]
        if stream == 2:
            return g1.at[rot(z, o), rot(y, -s)]
        return g1.at[rot(z, o), rot(y, s)]

    def forward(stream, s, j):
        to = ({"z": rot(z, 1)}, {"z": rot(z, -1)}, {"y": rot(y, 1)}, {"y": rot(y, -1)})[stream]
        block = unit(stream, s, j)
        remote(block, block, ring_send.at[stream], ring_recv.at[stream, s * N + j], **to)

    def came(stream, s, j):
        arrived(unit(stream, s + 1, j), ring_recv.at[stream, s * N + j])

    for stream in range(4):
        forward(stream, 0, 0)

    def level0(j, carry):
        o = offset_of(j)
        arrived(g0.at[z, rot(y, o)], p_recv.at[0, j])
        forward(0, 0, j)
        forward(1, 0, j)
        arrived(g1.at[rot(z, o), y], p_recv.at[1, j])
        forward(2, 0, j)
        forward(3, 0, j)
        return carry

    lax.fori_loop(1, N, level0, 0)

    def w1_wait(d, carry):
        zs = rot(z, -d)
        arrived(s1.at[zs], w1_recv.at[d])
        return carry

    own_w.wait()
    lax.fori_loop(1, N, w1_wait, 0)

    def w2_step(d, carry):
        yt = rot(y, d)
        remote(
            s1.at[:, :, pl.ds(pl.multiple_of(yt * 128, 128), 128)], wbuf.at[:, y, c], w_send.at[1], w2_recv.at[d], y=yt
        )
        return carry

    lax.fori_loop(1, N, w2_step, 0)
    own_w2 = pltpu.make_async_copy(
        s1.at[:, :, pl.ds(pl.multiple_of(y * 128, 128), 128)], wbuf.at[:, y, c], in_sem.at[7]
    )
    own_w2.start()

    def ring_step(k, carry):
        s, j = k // N, k % N
        for stream in range(4):
            came(stream, s - 1, j)
            forward(stream, s, j)
        return carry

    lax.fori_loop(N, 2 * N, ring_step, 0)

    def w2_wait(d, carry):
        arrived(wbuf.at[:, rot(y, -d), c], w2_recv.at[d])
        return carry

    own_w2.wait()
    lax.fori_loop(1, N, w2_wait, 0)
    remote(wbuf.at[:, :, c], wbuf.at[:, :, c], w_send.at[2], w3_recv, c=other)

    lax.fori_loop(2 * N, 3 * N, ring_step, 0)

    def last_step(j, carry):
        for stream in (0, 2):
            came(stream, 2, j)
            forward(stream, 3, j)
        for stream in (1, 3):
            came(stream, 2, j + 4)
            forward(stream, 3, j + 4)
        return carry

    lax.fori_loop(0, N // 2, last_step, 0)

    arrived(wbuf.at[:, :, other], w3_recv)
    wf[...] = wbuf[...].astype(F32).reshape(1024, 128)
    left = iota((128, 128), 1) < 64
    for h in range(8):
        part = wf[pl.ds(h, 128, stride=8), :]
        turned = pltpu.roll(part, 64, 1)
        w4[h * 128 : h * 128 + 128, 0:128] = jnp.where(left, part, turned).astype(BF16)
        w4[h * 128 : h * 128 + 128, 128:256] = jnp.where(left, turned, part).astype(BF16)

    def last_wait(j, carry):
        for stream in (0, 2):
            came(stream, 2, j + 4)
            came(stream, 3, j)
        for stream in (1, 3):
            came(stream, 2, j)
            came(stream, 3, j + 4)
        return carry

    lax.fori_loop(0, N // 2, last_wait, 0)

    half = iota((64, 128), 1) < 64
    for d in (4, 3, 5, 2, 6, 1, 7, 0):
        xt = rot(x, d)
        part = dot(g0[xt].reshape(128, 512), w4[0:512]) + dot(g1[xt].reshape(128, 512), w4[512:1024])
        top, bottom = part[0:64], part[64:128]
        to0 = jnp.where(half, top[:, 0:128], bottom[:, 0:128]).astype(BF16)
        to1 = jnp.where(half, top[:, 128:256], bottom[:, 128:256]).astype(BF16)
        cs[0, xt] = to0
        cs[1, xt] = to1
        if d:
            remote(cs.at[0, xt], cr.at[x * 2 + c], c_send, c_recv.at[2 * d + c], x=xt, c=0)
            remote(cs.at[1, xt], cr.at[x * 2 + c], c_send, c_recv.at[2 * d + c], x=xt, c=1)
        else:
            remote(cs.at[other, x], cr.at[x * 2 + c], c_send, c_recv.at[c], c=other)
            cr[x * 2 + c] = cs[c, x]

    loads[3].wait()
    loads[4].wait()
    loads[5].wait()
    row = iota((128, ROWS), 0)
    owner = (row % 64) * 2 + row // 64
    mine = (own_v[...] == owner).astype(F32)
    earlier = (iota((ROWS, ROWS), 0) < iota((ROWS, ROWS), 1)).astype(F32).astype(BF16)
    before = dot(mine.astype(BF16), earlier)
    slot = jnp.where(before == x.astype(F32), mine, F32(0)) * fin_v[...].astype(F32)
    oh[...] = slot.astype(BF16)
    base = base_v[...].astype(F32)
    base = jnp.concatenate([base[0:32], base[32:64]], axis=1)
    a, b = iota((128, 128), 0), iota((128, 128), 1)
    source = (a // 4 % 2) * 64 + (a // 8 % 4) * 16 + (a // 32) * 4 + a % 4
    order = (b == source).astype(F32).astype(BF16)

    def c_wait(d, carry):
        arrived(cr.at[rot(x, -d) * 2], c_recv.at[2 * d])
        arrived(cr.at[rot(x, -d) * 2 + 1], c_recv.at[2 * d + 1])
        return carry

    arrived(cr.at[x * 2 + other], c_recv.at[other])
    lax.fori_loop(1, N, c_wait, 0)
    summed = cr[pl.ds(0, 2)].astype(F32)
    for i in range(1, N):
        summed = summed + cr[pl.ds(2 * i, 2)].astype(F32)
    rows = dot(order, summed.reshape(128, 128).astype(BF16))
    stream = base + (((rows[0:32] + rows[32:64]) + rows[64:96]) + rows[96:128])
    sp[...] = stream.astype(BF16)

    def s_step(d, carry):
        remote(sp, sg.at[x], s_send, s_recv.at[d], x=rot(x, d))
        return carry

    lax.fori_loop(1, N, s_step, 0)
    sg[x] = sp[...]
    turned = pltpu.roll(rows, 64, 1)
    for t in range(4):
        uout[t, 0:32, :] = rows[t * 32 : t * 32 + 32, 0:64].astype(BF16)
        uout[t, 32:64, :] = turned[t * 32 : t * 32 + 32, 0:64].astype(BF16)
    save_updates = pltpu.make_async_copy(uout, upd_hbm, out_sem.at[0])
    save_updates.start()

    def s_wait(d, carry):
        arrived(sg.at[rot(x, -d)], s_recv.at[d])
        return carry

    lax.fori_loop(1, N, s_wait, 0)

    for i in range(N):
        block = sg[i].astype(F32)
        sgu[i * 64 : i * 64 + 32, :] = block.astype(BF16)
        sgu[i * 64 + 32 : i * 64 + 64, :] = pltpu.roll(block, 64, 1).astype(BF16)
    chosen = dot(oh[...], sgu[...])
    packed = jnp.where(half, chosen[0:64], pltpu.roll(chosen[64:128], 64, 1))
    o1[...] = packed.reshape(8, 8, 128).astype(BF16)

    def z_step(d, carry):
        zt = rot(z, d)
        remote(o1.at[zt], r1.at[z], z_send, z_recv.at[d], z=zt)
        return carry

    lax.fori_loop(1, N, z_step, 0)
    r1[z] = o1[z]

    def z_wait(d, carry):
        arrived(r1.at[rot(z, -d)], z_recv.at[d])
        return carry

    lax.fori_loop(1, N, z_wait, 0)
    tf[...] = r1[...].astype(F32).reshape(64, 128)
    for i in range(N):
        t2[i] = tf[pl.ds(i, 8, stride=8), :].astype(BF16)

    def y_step(d, carry):
        yt = rot(y, d)
        remote(t2.at[yt], r2.at[y * 2 + c], y_send, y_recv.at[2 * d + c], y=yt, c=0)
        remote(t2.at[yt], r2.at[y * 2 + c], y_send, y_recv.at[2 * d + c], y=yt, c=1)
        return carry

    remote(t2.at[y], r2.at[y * 2 + c], y_send, y_recv.at[c], c=other)
    lax.fori_loop(1, N, y_step, 0)
    r2[y * 2 + c] = t2[y]

    def y_wait(d, carry):
        arrived(r2.at[rot(y, -d) * 2], y_recv.at[2 * d])
        arrived(r2.at[rot(y, -d) * 2 + 1], y_recv.at[2 * d + 1])
        return carry

    arrived(r2.at[y * 2 + other], y_recv.at[other])
    lax.fori_loop(1, N, y_wait, 0)
    eighth = iota((8, 128), 1) < 64
    for i in range(N):
        v0, v1 = r2[2 * i].astype(F32), r2[2 * i + 1].astype(F32)
        a0 = jnp.where(c == 0, v0, pltpu.roll(v0, 64, 1))
        a1 = jnp.where(c == 0, pltpu.roll(v1, 64, 1), v1)
        tf[i * 8 : i * 8 + 8, :] = jnp.where(eighth, a0, a1)
    for i in range(N):
        trout[i * 8 : i * 8 + 8, :] = tf[pl.ds(i, 8, stride=8), :].astype(BF16)
    save_rows = pltpu.make_async_copy(trout, tr_hbm, out_sem.at[1])
    save_rows.start()

    arrived(s1.at[pl.ds(0, 7)], w_send.at[0])
    arrived(s1.at[pl.ds(0, 7)], w_send.at[1])
    arrived(wbuf.at[:, :, c], w_send.at[2])
    arrived(g0.at[0, pl.ds(0, 7)], p_send.at[0])
    arrived(g0.at[0, pl.ds(0, 7)], p_send.at[1])
    for i in range(4):
        arrived(g0.at[pl.ds(0, 7), pl.ds(0, 4)], ring_send.at[i])
    arrived(cr.at[pl.ds(0, 15)], c_send)
    arrived(sg.at[pl.ds(0, 7)], s_send)
    arrived(r1.at[pl.ds(0, 7)], z_send)
    arrived(r2.at[pl.ds(0, 15)], y_send)
    save_updates.wait()
    save_rows.wait()


def shards(base_stream, out_weight, queries, cache_keys, cache_values, new_keys, new_values, lengths, finished, owners):
    hbm = pl.BlockSpec(memory_space=pl.ANY)
    dma = pltpu.SemaphoreType.DMA
    updates, rows = pl.pallas_call(
        kernel,
        out_shape=(jax.ShapeDtypeStruct((4, 64, 64), BF16), jax.ShapeDtypeStruct((64, 128), BF16)),
        in_specs=[pl.BlockSpec(memory_space=pltpu.SMEM)] + [hbm] * 9,
        out_specs=(hbm, hbm),
        scratch_shapes=[
            pltpu.VMEM((4, 4, 8, 128), BF16),
            pltpu.VMEM((4, FULL, 128), BF16),
            pltpu.VMEM((4, FULL, 128), BF16),
            pltpu.VMEM((16, 128), BF16),
            pltpu.VMEM((16, 128), BF16),
            pltpu.VMEM((64, 64), BF16),
            pltpu.VMEM((1, ROWS), I32),
            pltpu.VMEM((1, ROWS), I32),
            pltpu.VMEM((8, 8, 1024), BF16),
            pltpu.VMEM((8, 8, 2, 8, 128), BF16),
            pltpu.VMEM((1024, 128), F32),
            pltpu.VMEM((1024, 256), BF16),
            pltpu.VMEM((128, 128), F32),
            pltpu.VMEM((8, 8, 16, 512), BF16),
            pltpu.VMEM((8, 8, 16, 512), BF16),
            pltpu.VMEM((2, 8, 64, 128), BF16),
            pltpu.VMEM((16, 64, 128), BF16),
            pltpu.VMEM((32, 128), BF16),
            pltpu.VMEM((8, 32, 128), BF16),
            pltpu.VMEM((ROWS, 128), BF16),
            pltpu.VMEM((128, ROWS), BF16),
            pltpu.VMEM((8, 8, 128), BF16),
            pltpu.VMEM((8, 8, 128), BF16),
            pltpu.VMEM((64, 128), F32),
            pltpu.VMEM((8, 8, 128), BF16),
            pltpu.VMEM((16, 8, 128), BF16),
            pltpu.VMEM((4, 64, 64), BF16),
            pltpu.VMEM((64, 128), BF16),
            dma((8,)),
            dma((2, 4)),
            dma((2,)),
            dma((3,)),
            dma((8,)),
            dma((8,)),
            dma,
            dma((2,)),
            dma((2, 8)),
            dma((4,)),
            dma((4, 32)),
            dma,
            dma((16,)),
            dma,
            dma((8,)),
            dma,
            dma((8,)),
            dma,
            dma((16,)),
        ],
        compiler_params=pltpu.CompilerParams(collective_id=0, has_side_effects=True),
        name="decode",
    )(
        lengths,
        queries,
        cache_keys.reshape(4, CTX, 128),
        cache_values.reshape(4, CTX, 128),
        new_keys.reshape(16, 128),
        new_values.reshape(16, 128),
        out_weight.reshape(8, 8192),
        base_stream,
        owners.reshape(1, ROWS),
        finished.reshape(1, ROWS),
    )
    return updates, rows.reshape(1, 1, 8192)


def solution(mesh):
    torus = Mesh(mesh.devices.reshape(N, N, 2, N), (ZA, YA, CA, XA))
    placed = (
        P(XA, REPLICA),
        P(XA, REPLICA, None),
        P(None, REPLICA, XA, None),
        P(REPLICA, XA, None, None),
        P(REPLICA, XA, None, None),
        P(None, REPLICA, XA, None),
        P(None, REPLICA, XA, None),
        P(REPLICA),
        P(),
        P(),
    )
    return jax.shard_map(
        shards, mesh=torus, in_specs=placed, out_specs=(P(None, XA, REPLICA), P(REPLICA, XA, None)), check_vma=False
    )
```

time: 216 us -> 75 us (0.35)
  waiting for transfers between devices: 119 us -> 0 us
  Pallas kernels: 0 us -> 71.3 us
  blocking collectives: 39.4 us -> 0 us
  starting transfers between devices: 24.8 us -> 0 us
  between operations: 14.3 us -> 0.64 us
  matrix products: 8.95 us -> 0 us
  other arithmetic: 3.91 us -> 0 us
  local copies, waits for them, and re-layouts: 5.74 us -> 2.82 us
    all_gather x2 -> x0, waiting for transfers between devices: 101 us -> none  [the longest x1 63.9 us: shards(): lax.all_gather(attended, REPLICA, axis=1, tiled=True)]
    pallas_call x0 -> x1, Pallas kernels: none -> 71.3 us  [shards(): pl.pallas_call(kernel, out_shape=(jax.ShapeDtypeStruct((4, 64, 64), BF16)...]
    all_to_all x2 -> x0, blocking collectives: 39.4 us -> none  [turned_blocks(): result = lax.all_to_all(result, axes[k], k, k, tiled=True)]
    all_to_all x2 -> x0, starting transfers between devices: 24.7 us -> none  [the longest x1 21 us: shards(): lax.all_to_all(outgoing, REPLICA, split_axis=0, concat_axis=2, tiled=True)]
    all_to_all x2 -> x0, waiting for transfers between devices: 18 us -> none  [the longest x1 10.7 us: shards(): lax.all_to_all(outgoing, REPLICA, split_axis=0, concat_axis=2, tiled=True)]
    dot_general x6 -> x0, matrix products: 8.95 us -> none  [the longest x1 5.37 us: shards(): jnp.einsum('tbf,fc->tbc', lax.all_gather(attended, REPLICA, axis=1, tiled...]
    reduce_sum x5 -> x0, other arithmetic: 2.55 us -> none  [the longest x1 1.9 us: gathered_total(): return pieces.sum(axis=0)]
  transfers between devices with their start and end apart: 4 -> 0, of which waited for: 4 -> 0; matrix products, arithmetic and copies ran while one was open for 1% -> 0% of each run, Pallas kernels for 0% -> 0%
where the time goes in v1:
time: 75 us; the launch traced here: 74.8 us
  Pallas kernels  71.3 us (95%)
  local copies, waits for them, and re-layouts  2.82 us (4%)
    pallas_call x1, Pallas kernels, shards(): pl.pallas_call(kernel, out_shape=(jax.ShapeDtypeStruct((4, 64, 64), BF16)...  71.3 us

profile of v1, /device:TPU:1, one launch (start us, length us, event | category | flops | bytes accessed | tf_op | source)
XLA Modules:
  0.0 74.8 jit_solution(4109151707799289792)
XLA Ops:
  0.6 71.3 %decode.1 = (bf16[4,64,64]{2,1,0:T(8,128)(2,1)}, bf16[64,128]{1,0:T(8,128)(2,1)}) custom-call(s32[4]{0:T(128)} %len_ref.1, bf16[4,4,8,128]{3,2,1,0:T(8,128)(2,1)} %q_hbm.1, bf16[4,1536,128]{2,1,0:T(8,128)(2,1)} %bitcast.7, bf16[4,1536,128]{2,1,0:T(8,128)(2,1)} %bitcast.8, bf16[16,128]{1,0:T(8,128)(2,1)} %bitcast.10, bf16[16,128]{1,0:T(8,128)(2,1)} %bitcast.11, ...), custom_call_target="tpu_custom_call" | custom-call | tf_op jit(solution)/shard_map/decode/pallas_call | solution.py:392
  72.0 1.3 %reshape.35 = bf16[1,1,8192]{2,1,0:T(2,128)(2,1)} reshape(bf16[64,128]{1,0:T(8,128)(2,1)} %get-tuple-element.5) | data formatting | bytes 32768 | tf_op jit(solution)/shard_map/reshape | solution.py:460
  73.3 1.5 %copy.13 = bf16[4,64,64]{2,1,0:T(8,128)(2,1)} copy(bf16[4,64,64]{2,1,0:T(8,128)(2,1)} %get-tuple-element.8) | data formatting | bytes 65536

commit v2 on v1

v2 whole, which is shorter than its diff:
```python
import functools
import math

import jax
import jax.numpy as jnp
from jax import lax
from jax.experimental import pallas as pl
from jax.experimental.pallas import tpu as pltpu
from jax.sharding import Mesh
from jax.sharding import PartitionSpec as P

ZA, YA, CA, XA = "replica_0", "replica_1", "replica_2", "tensor"
REPLICA = (ZA, YA, CA)
MESH = pl.DeviceIdType.MESH
F32, BF16, I32 = jnp.float32, jnp.bfloat16, jnp.int32
N = 8
CTX = 1536
PAD = 128
FULL = CTX + PAD
ROWS = 512


def dot(a, b):
    return jnp.dot(a, b, preferred_element_type=F32)


def iota(shape, dim):
    return lax.broadcasted_iota(I32, shape, dim)


def offset_of(j):
    return (j + 1) // 2 * (2 * (j % 2) - 1)


def mirror(j):
    if j == 0 or j == N - 1:
        return j
    return j + 1 if j % 2 else j - 1


def kernel(
    len_hbm, q_hbm, k_hbm, v_hbm, nk_hbm, nv_hbm, w_hbm, base_hbm, own_hbm, fin_hbm,
    rows_out, r2,
    len_s, q_v, k_v, v_v, nk_v, nv_v, base_v, own_v, fin_v,
    sa, sb, wbuf, wf, w4, att, g0, g1, part0, part1, pn, ts, tr, cs, cr, bp, bg, sgu, oh, o1, r1, tf, t2,
    in_sem, kv_sem,
    w_send, w1_recv, w2_recv, w3_recv,
    p_send, p_recv, ring_send, ring_recv,
    t_send, t_recv, c_send, c_recv, b_send, b_recv, z_send, z_recv, y_send, y_recv,
):
    z, y, c, x = (lax.axis_index(a) for a in (ZA, YA, CA, XA))
    other = 1 - c

    def rot(i, d):
        return lax.rem(i + d + N, N)

    def remote(src, dst, ssem, rsem, **to):
        pltpu.make_async_remote_copy(
            src_ref=src, dst_ref=dst, send_sem=ssem, recv_sem=rsem,
            device_id={{"z": ZA, "y": YA, "c": CA, "x": XA}[k]: v for k, v in to.items()},
            device_id_type=MESH,
        ).start()

    def arrived(ref, sem):
        pltpu.make_async_copy(ref, ref, sem).wait()

    small = [
        (q_hbm, q_v), (nk_hbm, nk_v), (nv_hbm, nv_v), (len_hbm, len_s),
        (base_hbm, base_v), (own_hbm, own_v), (fin_hbm, fin_v),
    ]
    loads = [pltpu.make_async_copy(a, b, in_sem.at[i]) for i, (a, b) in enumerate(small)]
    k_loads = [pltpu.make_async_copy(k_hbm.at[b], k_v.at[b, pl.ds(0, CTX)], kv_sem.at[0, b]) for b in range(4)]
    v_loads = [pltpu.make_async_copy(v_hbm.at[b], v_v.at[b, pl.ds(0, CTX)], kv_sem.at[1, b]) for b in range(4)]
    for load in loads[:4]:
        load.start()
    for b in range(4):
        k_loads[b].start()
        v_loads[b].start()
    for load in loads[4:]:
        load.start()

    barrier = pltpu.get_barrier_semaphore()

    def greet(**to):
        pl.semaphore_signal(
            barrier, inc=1, device_id={{"z": ZA, "y": YA, "c": CA, "x": XA}[k]: v for k, v in to.items()},
            device_id_type=MESH,
        )

    greet(c=other)

    def greet_step(d, carry):
        greet(z=rot(z, d))
        greet(y=rot(y, d), c=0)
        greet(y=rot(y, d), c=1)
        greet(x=rot(x, d), c=0)
        greet(x=rot(x, d), c=1)
        return carry

    lax.fori_loop(1, N, greet_step, 0)

    for load in loads[:4]:
        load.wait()
    nk, nv = nk_v[...], nv_v[...]
    for b in range(4):
        pick = (iota((PAD, 16), 1) == iota((PAD, 16), 0) * 4 + b).astype(F32).astype(BF16)
        k_v[b, CTX:FULL, :] = dot(pick, nk).astype(BF16)
        v_v[b, CTX:FULL, :] = dot(pick, nv).astype(BF16)

    scale = 1.0 / math.sqrt(128.0)

    def attend(b):
        q = q_v[:, b].astype(F32).reshape(32, 128).astype(BF16)
        k_loads[b].wait()
        scores = lax.dot_general(q, k_v[b], (((1,), (1,)), ((), ())), preferred_element_type=F32) * scale
        col = iota((32, FULL), 1)
        step = iota((32, FULL), 0) // 8
        keep = (col < len_s[b]) | ((col >= CTX) & (col - CTX <= step))
        scores = jnp.where(keep, scores, F32(-1e30))
        high = jnp.max(scores, axis=-1, keepdims=True)
        weight = jnp.exp(scores - high)
        total = jnp.sum(weight, axis=-1, keepdims=True)
        probs = (weight / total).astype(BF16)
        v_loads[b].wait()
        mixed = dot(probs, v_v[b])
        for t in range(4):
            att[pl.ds((t * 4 + b) * 8, 8), :] = mixed[t * 8 : t * 8 + 8]

    attend(0)
    attend(1)
    attend(2)
    pl.semaphore_wait(barrier, 5 * (N - 1) + 1)

    def via_z(zt):
        return w_hbm.at[zt // 2, zt % 2, :, zt % 2]

    def via_y(yt):
        return w_hbm.at[:, (yt + 1) % 2, yt // 2, yt % 2]

    own_w = [
        pltpu.make_async_copy(via_z(z), sa.at[z], in_sem.at[7]),
        pltpu.make_async_copy(via_y(y), sb.at[y], in_sem.at[8]),
    ]
    for load in own_w:
        load.start()

    def w1_step(d, carry):
        zt, yt = rot(z, d), rot(y, d)
        remote(via_z(zt), sa.at[z], w_send.at[0], w1_recv, z=zt)
        remote(via_y(yt), sb.at[y], w_send.at[0], w1_recv, y=yt)
        return carry

    lax.fori_loop(1, N, w1_step, 0)

    for load in loads[4:]:
        load.wait()
    base = base_v[...].astype(F32)
    bp[...] = jnp.concatenate([base[0:32], base[32:64]], axis=1).astype(BF16)

    def base_step(d, carry):
        remote(bp, bg.at[x], b_send, b_recv, x=rot(x, d))
        return carry

    lax.fori_loop(1, N, base_step, 0)
    bg[x] = bp[...]
    attend(3)
    for h in range(8):
        part = att[pl.ds(h, 16, stride=8), :].astype(BF16)
        (g0 if h < 4 else g1)[z, y, :, (h % 4) * 128 : (h % 4) * 128 + 128] = part

    for j in range(1, N):
        o = offset_of(j)
        remote(g0.at[z, y], g0.at[z, y], p_send.at[0], p_recv.at[0, mirror(j) // 2], y=rot(y, o))
        remote(g1.at[z, y], g1.at[z, y], p_send.at[1], p_recv.at[1, mirror(j) // 2], z=rot(z, o))

    def unit(stream, s, j):
        o = offset_of(j)
        if stream == 0:
            return g0.at[rot(z, -s), rot(y, o)]
        if stream == 1:
            return g0.at[rot(z, s), rot(y, o)]
        if stream == 2:
            return g1.at[rot(z, o), rot(y, -s)]
        return g1.at[rot(z, o), rot(y, s)]

    def slot_of(s, pair):
        return s * 4 + (pair % 2 if isinstance(s, int) and s == 3 else pair)

    def forward(stream, s, pair, places=(0, 1)):
        to = ({"z": rot(z, 1)}, {"z": rot(z, -1)}, {"y": rot(y, 1)}, {"y": rot(y, -1)})[stream]
        for i in places:
            block = unit(stream, s, pair * 2 + i)
            remote(block, block, ring_send.at[stream], ring_recv.at[stream, slot_of(s, pair)], **to)

    def came(stream, s, pair):
        arrived(g0.at[0, pl.ds(0, 2)], ring_recv.at[stream, slot_of(s, pair)])

    for stream in range(4):
        forward(stream, 0, 0, (0,))

    def level0(pair):
        for half_of in range(2):
            arrived(g0.at[0, pl.ds(0, 2 if pair else 1)], p_recv.at[half_of, pair])
            for stream in (2 * half_of, 2 * half_of + 1):
                forward(stream, 0, pair, (0, 1) if pair else (1,))

    level0(0)
    level0(1)

    for load in own_w:
        load.wait()
    arrived(g0.at[0, pl.ds(0, 7)], w1_recv)
    even = (z + y) % 2 == 0

    def w2_step(i, carry):
        yt, zt = 2 * i + z % 2, 2 * i + (y + 1) % 2

        @pl.when(yt != y)
        def _():
            remote(sa.at[:, i], wbuf.at[:, y, c], w_send.at[0], w2_recv, y=yt)

        @pl.when(zt != z)
        def _():
            remote(sb.at[:, i], wbuf.at[z, :, c], w_send.at[0], w2_recv, z=zt)

        return carry

    lax.fori_loop(0, N // 2, w2_step, 0)

    @pl.when(even)
    def _():
        pltpu.make_async_copy(sa.at[:, y // 2], wbuf.at[:, y, c], in_sem.at[9]).start()

    @pl.when(jnp.logical_not(even))
    def _():
        pltpu.make_async_copy(sb.at[:, z // 2], wbuf.at[z, :, c], in_sem.at[9]).start()

    level0(2)
    level0(3)

    def ring_step(k, carry):
        s, pair = k // 4, k % 4
        for stream in range(4):
            came(stream, s - 1, pair)
            forward(stream, s, pair)
        return carry

    lax.fori_loop(4, 12, ring_step, 0)

    arrived(g0.at[0, pl.ds(0, 1)], in_sem.at[9])
    arrived(g0.at[0, pl.ds(0, 7)], w2_recv)
    remote(wbuf.at[:, :, c], wbuf.at[:, :, c], w_send.at[1], w3_recv, c=other)

    for pair in range(2):
        for stream in range(4):
            mine_of = pair + 2 * (stream % 2)
            came(stream, 2, mine_of)
            forward(stream, 3, mine_of)

    for pair in range(2):
        for stream in range(4):
            came(stream, 2, pair + 2 * (1 - stream % 2))

    arrived(wbuf.at[:, :, other], w3_recv)
    wf[...] = wbuf[...].astype(F32).reshape(1024, 128)
    left = iota((128, 128), 1) < 64
    for h in range(8):
        part = wf[pl.ds(h, 128, stride=8), :]
        turned = pltpu.roll(part, 64, 1)
        w4[h * 128 : h * 128 + 128, 0:128] = jnp.where(left, part, turned).astype(BF16)
        w4[h * 128 : h * 128 + 128, 128:256] = jnp.where(left, turned, part).astype(BF16)

    def product0(d):
        zt = rot(z, d)
        part0[zt] = dot(g0[zt].reshape(128, 512), w4[0:512]).reshape(8, 16, 256)

    def product1(d):
        yt = rot(y, d)
        part1[yt] = dot(g1[:, yt].reshape(128, 512), w4[512:1024]).reshape(8, 16, 256)

    for d in (0, 1, 2, 3, 5, 6, 7):
        product0(d)
        product1(d)
    row = iota((128, ROWS), 0)
    owner = (row % 64) * 2 + row // 64
    mine = (own_v[...] == owner).astype(F32)
    earlier = (iota((ROWS, ROWS), 0) < iota((ROWS, ROWS), 1)).astype(F32).astype(BF16)
    before = dot(mine.astype(BF16), earlier)
    mine = mine * fin_v[...].astype(F32)
    for i in range(N):
        oh[i] = jnp.where(before == F32(i), mine, F32(0)).astype(BF16)
    a, b = iota((128, 128), 0), iota((128, 128), 1)
    source = (a // 4 % 2) * 64 + (a // 8 % 4) * 16 + (a // 32) * 4 + a % 4
    order = (b == source).astype(F32).astype(BF16)

    for pair in range(2):
        for stream in range(4):
            came(stream, 3, pair + 2 * (stream % 2))
    product0(4)
    product1(4)

    left8 = iota((8, 8, 128), 2) < 64
    own8 = iota((8, 8, 128), 1) // 4 == c
    for i in range(N):
        block = part0[i] + part1[:, i]
        block = block[:, 0:8] + block[:, 8:16]
        block = jnp.where(left8, block[:, :, 0:128], block[:, :, 128:256])
        block = jnp.where(own8, block + pltpu.roll(block, 4, 1), F32(0))
        pn[i * 64 : i * 64 + 64, :] = block.reshape(64, 128).astype(BF16)

    half = iota((64, 128), 1) < 64
    for d in (4, 3, 5, 2, 6, 1, 7, 0):
        xt = rot(x, d)
        chosen = dot(oh[xt], pn[...])
        first, second = chosen[0:64], chosen[64:128]
        ts[0, xt] = jnp.where(half, first, pltpu.roll(second, 64, 1)).astype(BF16)
        ts[1, xt] = jnp.where(half, pltpu.roll(first, 64, 1), second).astype(BF16)
        if d:
            remote(ts.at[0, xt], tr.at[x * 2 + c], t_send, t_recv, x=xt, c=0)
            remote(ts.at[1, xt], tr.at[x * 2 + c], t_send, t_recv, x=xt, c=1)
        else:
            remote(ts.at[other, x], tr.at[x * 2 + c], t_send, t_recv, c=other)
            tr[x * 2 + c] = ts[c, x]

    arrived(bg.at[pl.ds(0, 7)], b_recv)
    for i in range(N):
        block = bg[i].astype(F32)
        sgu[i * 64 : i * 64 + 32, :] = block.astype(BF16)
        sgu[i * 64 + 32 : i * 64 + 64, :] = pltpu.roll(block, 64, 1).astype(BF16)
    chosen = dot(oh[x], sgu[...])
    total = jnp.where(half, chosen[0:64], pltpu.roll(chosen[64:128], 64, 1))

    arrived(tr.at[pl.ds(0, 15)], t_recv)
    summed = tr[0].astype(F32)
    for i in range(1, 2 * N):
        summed = summed + tr[i].astype(F32)
    o1[...] = (total + summed).reshape(8, 8, 128).astype(BF16)

    def z_step(d, carry):
        zt = rot(z, d)
        remote(o1.at[zt], r1.at[z], z_send, z_recv, z=zt)
        return carry

    lax.fori_loop(1, N, z_step, 0)
    r1[z] = o1[z]

    for d in (4, 3, 5, 2, 6, 1, 7, 0):
        xt = rot(x, d)
        part = (part0[xt] + part1[:, xt]).reshape(128, 256)
        top, bottom = part[0:64], part[64:128]
        cs[0, xt] = jnp.where(half, top[:, 0:128], bottom[:, 0:128]).astype(BF16)
        cs[1, xt] = jnp.where(half, top[:, 128:256], bottom[:, 128:256]).astype(BF16)
        if d:
            remote(cs.at[0, xt], cr.at[x * 2 + c], c_send, c_recv, x=xt, c=0)
            remote(cs.at[1, xt], cr.at[x * 2 + c], c_send, c_recv, x=xt, c=1)
        else:
            remote(cs.at[other, x], cr.at[x * 2 + c], c_send, c_recv, c=other)
            cr[x * 2 + c] = cs[c, x]

    arrived(r1.at[pl.ds(0, 7)], z_recv)
    tf[...] = r1[...].astype(F32).reshape(64, 128)
    for i in range(N):
        t2[i] = tf[pl.ds(i, 8, stride=8), :].astype(BF16)

    def y_step(d, carry):
        yt = rot(y, d)
        remote(t2.at[yt], r2.at[y * 2 + c], y_send, y_recv, y=yt, c=0)
        remote(t2.at[yt], r2.at[y * 2 + c], y_send, y_recv, y=yt, c=1)
        return carry

    remote(t2.at[y], r2.at[y * 2 + c], y_send, y_recv, c=other)
    lax.fori_loop(1, N, y_step, 0)
    r2[y * 2 + c] = t2[y]

    arrived(cr.at[pl.ds(0, 15)], c_recv)
    summed = cr[pl.ds(0, 2)].astype(F32)
    for i in range(1, N):
        summed = summed + cr[pl.ds(2 * i, 2)].astype(F32)
    rows_out[...] = dot(order, summed.reshape(128, 128).astype(BF16)).astype(BF16)

    arrived(r2.at[pl.ds(0, 15)], y_recv)

    arrived(g0.at[pl.ds(0, 7), pl.ds(0, 2)], w_send.at[0])
    arrived(wbuf.at[:, :, c], w_send.at[1])
    arrived(g0.at[0, pl.ds(0, 7)], p_send.at[0])
    arrived(g0.at[0, pl.ds(0, 7)], p_send.at[1])
    for i in range(4):
        arrived(g0.at[pl.ds(0, 7), pl.ds(0, 4)], ring_send.at[i])
    arrived(cr.at[pl.ds(0, 15)], c_send)
    arrived(bg.at[pl.ds(0, 7)], b_send)
    arrived(tr.at[pl.ds(0, 15)], t_send)
    arrived(r1.at[pl.ds(0, 7)], z_send)
    arrived(r2.at[pl.ds(0, 15)], y_send)


def finish(rows_ref, r2_ref, upd_ref, tr_ref, tf):
    c = lax.axis_index(CA)
    rows = rows_ref[...].astype(F32)
    turned = pltpu.roll(rows, 64, 1)
    for t in range(4):
        upd_ref[t, 0:32, :] = rows[t * 32 : t * 32 + 32, 0:64].astype(BF16)
        upd_ref[t, 32:64, :] = turned[t * 32 : t * 32 + 32, 0:64].astype(BF16)
    eighth = iota((8, 128), 1) < 64
    for i in range(N):
        v0, v1 = r2_ref[2 * i].astype(F32), r2_ref[2 * i + 1].astype(F32)
        a0 = jnp.where(c == 0, v0, pltpu.roll(v0, 64, 1))
        a1 = jnp.where(c == 0, pltpu.roll(v1, 64, 1), v1)
        tf[i * 8 : i * 8 + 8, :] = jnp.where(eighth, a0, a1)
    for i in range(N):
        block = tf[pl.ds(i, 8, stride=8), :]
        for k in range(N):
            at = (i * N + k) * 128
            tr_ref[0, :, at : at + 128] = block[k : k + 1].astype(BF16)


def shards(base_stream, out_weight, queries, cache_keys, cache_values, new_keys, new_values, lengths, finished, owners):
    hbm = pl.BlockSpec(memory_space=pltpu.HBM)
    vmem = pl.BlockSpec(memory_space=pltpu.VMEM)
    dma = pltpu.SemaphoreType.DMA
    rows, handed = pl.pallas_call(
        kernel,
        out_shape=(jax.ShapeDtypeStruct((128, 128), BF16), jax.ShapeDtypeStruct((16, 8, 128), BF16)),
        in_specs=[hbm] * 10,
        out_specs=(vmem, vmem),
        scratch_shapes=[
            pltpu.SMEM((4,), I32),
            pltpu.VMEM((4, 4, 8, 128), BF16),
            pltpu.VMEM((4, FULL, 128), BF16),
            pltpu.VMEM((4, FULL, 128), BF16),
            pltpu.VMEM((16, 128), BF16),
            pltpu.VMEM((16, 128), BF16),
            pltpu.VMEM((64, 64), BF16),
            pltpu.VMEM((1, ROWS), I32),
            pltpu.VMEM((1, ROWS), I32),
            pltpu.VMEM((8, 4, 8, 128), BF16),
            pltpu.VMEM((8, 4, 8, 128), BF16),
            pltpu.VMEM((8, 8, 2, 8, 128), BF16),
            pltpu.VMEM((1024, 128), F32),
            pltpu.VMEM((1024, 256), BF16),
            pltpu.VMEM((128, 128), F32),
            pltpu.VMEM((8, 8, 16, 512), BF16),
            pltpu.VMEM((8, 8, 16, 512), BF16),
            pltpu.VMEM((8, 8, 16, 256), F32),
            pltpu.VMEM((8, 8, 16, 256), F32),
            pltpu.VMEM((ROWS, 128), BF16),
            pltpu.VMEM((2, 8, 64, 128), BF16),
            pltpu.VMEM((16, 64, 128), BF16),
            pltpu.VMEM((2, 8, 64, 128), BF16),
            pltpu.VMEM((16, 64, 128), BF16),
            pltpu.VMEM((32, 128), BF16),
            pltpu.VMEM((8, 32, 128), BF16),
            pltpu.VMEM((ROWS, 128), BF16),
            pltpu.VMEM((8, 128, ROWS), BF16),
            pltpu.VMEM((8, 8, 128), BF16),
            pltpu.VMEM((8, 8, 128), BF16),
            pltpu.VMEM((64, 128), F32),
            pltpu.VMEM((8, 8, 128), BF16),
            dma((10,)),
            dma((2, 4)),
            dma((2,)),
            dma,
            dma,
            dma,
            dma((2,)),
            dma((2, 4)),
            dma((4,)),
            dma((4, 14)),
            dma,
            dma,
            dma,
            dma,
            dma,
            dma,
            dma,
            dma,
            dma,
            dma,
        ],
        compiler_params=pltpu.CompilerParams(collective_id=0, has_side_effects=True, vmem_limit_bytes=24 << 20),
        name="decode",
    )(*(pltpu.with_memory_space_constraint(a, pltpu.HBM) for a in (
        lengths,
        queries,
        cache_keys.reshape(4, CTX, 128),
        cache_values.reshape(4, CTX, 128),
        new_keys.reshape(16, 128),
        new_values.reshape(16, 128),
        out_weight.reshape(8, 64, 128).transpose(1, 0, 2).reshape(4, 2, 4, 2, 8, 128),
        base_stream,
        owners.reshape(1, ROWS),
        finished.reshape(1, ROWS),
    )))
    return pl.pallas_call(
        finish,
        out_shape=(jax.ShapeDtypeStruct((4, 64, 64), BF16), jax.ShapeDtypeStruct((1, 1, 8192), BF16)),
        in_specs=[vmem, vmem],
        out_specs=(vmem, vmem),
        scratch_shapes=[pltpu.VMEM((64, 128), F32)],
        compiler_params=pltpu.CompilerParams(vmem_limit_bytes=4 << 20),
        name="finish",
    )(rows, handed)


def solution(mesh):
    torus = Mesh(mesh.devices.reshape(N, N, 2, N), (ZA, YA, CA, XA))
    placed = (
        P(XA, REPLICA),
        P(XA, REPLICA, None),
        P(None, REPLICA, XA, None),
        P(REPLICA, XA, None, None),
        P(REPLICA, XA, None, None),
        P(None, REPLICA, XA, None),
        P(None, REPLICA, XA, None),
        P(REPLICA),
        P(),
        P(),
    )
    return jax.shard_map(
        shards, mesh=torus, in_specs=placed, out_specs=(P(None, XA, REPLICA), P(REPLICA, XA, None)), check_vma=False
    )
```

time: 75 us -> 64.7 us (0.86)
  Pallas kernels: 71.3 us -> 64 us
  local copies, waits for them, and re-layouts: 2.82 us -> 0 us
    pallas_call x1 -> x2, Pallas kernels: 71.3 us -> 64 us  [the longest x1 63.2 us: shards(): pl.pallas_call(kernel, out_shape=(jax.ShapeDtypeStruct((128, 128), BF16),...]
    unnamed x1 -> x0, local copies, waits for them, and re-layouts: 1.47 us -> none
    reshape x1 -> x0, local copies, waits for them, and re-layouts: 1.34 us -> none  [shards(): return (updates, rows.reshape(1, 1, 8192))]
where the time goes in v2:
time: 64.7 us; the launch traced here: 64.6 us
  Pallas kernels  64 us (99%)
    pallas_call x1, Pallas kernels, shards(): pl.pallas_call(kernel, out_shape=(jax.ShapeDtypeStruct((128, 128), BF16),...  63.2 us

profile of v2, /device:TPU:1, one launch (start us, length us, event | category | flops | bytes accessed | tf_op | source)
XLA Modules:
  0.0 64.6 jit_solution(17814248062136460084)
XLA Ops:
  0.6 63.2 %decode.1 = (bf16[128,128]{1,0:T(8,128)(2,1)S(1)}, bf16[16,8,128]{2,1,0:T(8,128)(2,1)S(1)}) custom-call(s32[4]{0:T(128)} %len_hbm.1, bf16[4,4,8,128]{3,2,1,0:T(8,128)(2,1)} %q_hbm.1, bf16[4,1536,128]{2,1,0:T(8,128)(2,1)} %bitcast.11, bf16[4,1536,128]{2,1,0:T(8,128)(2,1)} %bitcast.12, bf16[16,128]{1,0:T(8,128)(2,1)} %bitcast.14, bf16[16,128]{1,0:T(8,128)(2,1)} %bitcast.15, ...), custom_call_target="tpu_custom_call" | custom-call | tf_op jit(solution)/shard_map/decode/pallas_call | solution.py:420
  63.8 0.8 %finish.1 = (bf16[4,64,64]{2,1,0:T(8,128)(2,1)}, bf16[1,1,8192]{2,1,0:T(2,128)(2,1)}) custom-call(bf16[128,128]{1,0:T(8,128)(2,1)S(1)} %get-tuple-element.4.rows_ref, bf16[16,8,128]{2,1,0:T(8,128)(2,1)S(1)} %get-tuple-element.5.r2_ref), custom_call_target="tpu_custom_call" | custom-call | tf_op jit(solution)/shard_map/finish/pallas_call | solution.py:493

commit v3 on v2

--- a/solution.py
+++ b/solution.py
@@ -18,6 +18,7 @@
 PAD = 128
 FULL = CTX + PAD
 ROWS = 512
+FAR_FIRST = (4, 3, 5, 2, 6, 1, 7, 0)
 
 
 def dot(a, b):
@@ -42,11 +43,11 @@
     len_hbm, q_hbm, k_hbm, v_hbm, nk_hbm, nv_hbm, w_hbm, base_hbm, own_hbm, fin_hbm,
     rows_out, r2,
     len_s, q_v, k_v, v_v, nk_v, nv_v, base_v, own_v, fin_v,
-    sa, sb, wbuf, wf, w4, att, g0, g1, part0, part1, pn, ts, tr, cs, cr, bp, bg, sgu, oh, o1, r1, tf, t2,
+    sa, sb, wbuf, wf, w4, att, g0, g1, part0, part1, vv, ps, pin, pn, ts, tr, cs, cr, oh, tf, t2,
     in_sem, kv_sem,
     w_send, w1_recv, w2_recv, w3_recv,
     p_send, p_recv, ring_send, ring_recv,
-    t_send, t_recv, c_send, c_recv, b_send, b_recv, z_send, z_recv, y_send, y_recv,
+    known, u_send, u_recv, t_send, t_recv, c_send, c_recv, y_send, y_recv,
 ):
     z, y, c, x = (lax.axis_index(a) for a in (ZA, YA, CA, XA))
     other = 1 - c
@@ -111,7 +112,6 @@
 
     def attend(b):
         q = q_v[:, b].astype(F32).reshape(32, 128).astype(BF16)
-        k_loads[b].wait()
         scores = lax.dot_general(q, k_v[b], (((1,), (1,)), ((), ())), preferred_element_type=F32) * scale
         col = iota((32, FULL), 1)
         step = iota((32, FULL), 0) // 8
@@ -121,52 +121,20 @@
         weight = jnp.exp(scores - high)
         total = jnp.sum(weight, axis=-1, keepdims=True)
         probs = (weight / total).astype(BF16)
-        v_loads[b].wait()
         mixed = dot(probs, v_v[b])
         for t in range(4):
             att[pl.ds((t * 4 + b) * 8, 8), :] = mixed[t * 8 : t * 8 + 8]
 
-    attend(0)
-    attend(1)
-    attend(2)
-    pl.semaphore_wait(barrier, 5 * (N - 1) + 1)
-
-    def via_z(zt):
-        return w_hbm.at[zt // 2, zt % 2, :, zt % 2]
-
-    def via_y(yt):
-        return w_hbm.at[:, (yt + 1) % 2, yt // 2, yt % 2]
-
-    own_w = [
-        pltpu.make_async_copy(via_z(z), sa.at[z], in_sem.at[7]),
-        pltpu.make_async_copy(via_y(y), sb.at[y], in_sem.at[8]),
-    ]
-    for load in own_w:
-        load.start()
-
-    def w1_step(d, carry):
-        zt, yt = rot(z, d), rot(y, d)
-        remote(via_z(zt), sa.at[z], w_send.at[0], w1_recv, z=zt)
-        remote(via_y(yt), sb.at[y], w_send.at[0], w1_recv, y=yt)
-        return carry
-
-    lax.fori_loop(1, N, w1_step, 0)
-
-    for load in loads[4:]:
-        load.wait()
-    base = base_v[...].astype(F32)
-    bp[...] = jnp.concatenate([base[0:32], base[32:64]], axis=1).astype(BF16)
-
-    def base_step(d, carry):
-        remote(bp, bg.at[x], b_send, b_recv, x=rot(x, d))
-        return carry
-
-    lax.fori_loop(1, N, base_step, 0)
-    bg[x] = bp[...]
-    attend(3)
+    for first in (0, 2):
+        for b in (first, first + 1):
+            k_loads[b].wait()
+            v_loads[b].wait()
+        attend(first)
+        attend(first + 1)
     for h in range(8):
         part = att[pl.ds(h, 16, stride=8), :].astype(BF16)
         (g0 if h < 4 else g1)[z, y, :, (h % 4) * 128 : (h % 4) * 128 + 128] = part
+    pl.semaphore_wait(barrier, 5 * (N - 1) + 1)
 
     for j in range(1, N):
         o = offset_of(j)
@@ -204,8 +172,39 @@
             for stream in (2 * half_of, 2 * half_of + 1):
                 forward(stream, 0, pair, (0, 1) if pair else (1,))
 
-    level0(0)
-    level0(1)
+    def via_z(zt):
+        return w_hbm.at[zt // 2, zt % 2, :, zt % 2]
+
+    def via_y(yt):
+        return w_hbm.at[:, (yt + 1) % 2, yt // 2, yt % 2]
+
+    own_w = [
+        pltpu.make_async_copy(via_z(z), sa.at[z], in_sem.at[7]),
+        pltpu.make_async_copy(via_y(y), sb.at[y], in_sem.at[8]),
+    ]
+    for load in own_w:
+        load.start()
+
+    def w1_step(d, carry):
+        zt, yt = rot(z, d), rot(y, d)
+        remote(via_z(zt), sa.at[z], w_send.at[0], w1_recv, z=zt)
+        remote(via_y(yt), sb.at[y], w_send.at[0], w1_recv, y=yt)
+        return carry
+
+    lax.fori_loop(1, N, w1_step, 0)
+
+    for pair in range(4):
+        level0(pair)
+
+    def known_step(d, carry):
+        for core in range(2):
+            pl.semaphore_signal(
+                known, inc=1, device_id={XA: rot(x, d), CA: core}, device_id_type=MESH
+            )
+        return carry
+
+    lax.fori_loop(1, N, known_step, 0)
+    pl.semaphore_signal(known, inc=1, device_id={CA: other}, device_id_type=MESH)
 
     for load in own_w:
         load.wait()
@@ -235,14 +234,13 @@
     def _():
         pltpu.make_async_copy(sb.at[:, z // 2], wbuf.at[z, :, c], in_sem.at[9]).start()
 
-    level0(2)
-    level0(3)
 
     def ring_step(k, carry):
         s, pair = k // 4, k % 4
         for stream in range(4):
-            came(stream, s - 1, pair)
-            forward(stream, s, pair)
+            at = (pair + s * (stream % 2)) % 4
+            came(stream, s - 1, at)
+            forward(stream, s, at)
         return carry
 
     lax.fori_loop(4, 12, ring_step, 0)
@@ -281,14 +279,16 @@
     for d in (0, 1, 2, 3, 5, 6, 7):
         product0(d)
         product1(d)
+    for load in loads[4:]:
+        load.wait()
     row = iota((128, ROWS), 0)
     owner = (row % 64) * 2 + row // 64
     mine = (own_v[...] == owner).astype(F32)
     earlier = (iota((ROWS, ROWS), 0) < iota((ROWS, ROWS), 1)).astype(F32).astype(BF16)
     before = dot(mine.astype(BF16), earlier)
     mine = mine * fin_v[...].astype(F32)
-    for i in range(N):
-        oh[i] = jnp.where(before == F32(i), mine, F32(0)).astype(BF16)
+    for i, d in enumerate(FAR_FIRST):
+        oh[i] = jnp.where(before == rot(x, d).astype(F32), mine, F32(0)).astype(BF16)
     a, b = iota((128, 128), 0), iota((128, 128), 1)
     source = (a // 4 % 2) * 64 + (a // 8 % 4) * 16 + (a // 32) * 4 + a % 4
     order = (b == source).astype(F32).astype(BF16)
@@ -299,52 +299,52 @@
     product0(4)
     product1(4)
 
+    base = base_v[...].astype(F32)
+    base = jnp.where(iota((64, 128), 1) // 64 == c, jnp.concatenate([base, base], axis=1), F32(0))
     left8 = iota((8, 8, 128), 2) < 64
     own8 = iota((8, 8, 128), 1) // 4 == c
+    low4 = iota((4, 8, 128), 1) < 4
     for i in range(N):
         block = part0[i] + part1[:, i]
         block = block[:, 0:8] + block[:, 8:16]
         block = jnp.where(left8, block[:, :, 0:128], block[:, :, 128:256])
-        block = jnp.where(own8, block + pltpu.roll(block, 4, 1), F32(0))
-        pn[i * 64 : i * 64 + 64, :] = block.reshape(64, 128).astype(BF16)
+        block = block + pltpu.roll(block, 4, 1)
+        vv[i] = block
+        block = block.reshape(4, 2, 8, 128)
+        ps[i] = jnp.where(low4, block[:, 0], block[:, 1]).astype(BF16)
+        if i % 4 == 3:
+            group = pl.ds(i - 3, 4)
+            remote(ps.at[group], pin.at[group], u_send, u_recv.at[i // 4], c=other)
+    pl.semaphore_wait(known, 2 * N - 1)
+    for i in range(N):
+        if i % 4 == 0:
+            arrived(pin.at[pl.ds(i, 4)], u_recv.at[i // 4])
+        theirs = pin[i].astype(F32)
+        turned = pltpu.roll(theirs, 4, 1)
+        theirs = jnp.stack([jnp.where(low4, theirs, turned), jnp.where(low4, turned, theirs)], axis=1)
+        block = jnp.where(own8, vv[i], theirs.reshape(8, 8, 128)).reshape(64, 128)
+        pn[i * 64 : i * 64 + 64, :] = (block + jnp.where(x == i, base, F32(0))).astype(BF16)
 
     half = iota((64, 128), 1) < 64
-    for d in (4, 3, 5, 2, 6, 1, 7, 0):
-        xt = rot(x, d)
-        chosen = dot(oh[xt], pn[...])
-        first, second = chosen[0:64], chosen[64:128]
-        ts[0, xt] = jnp.where(half, first, pltpu.roll(second, 64, 1)).astype(BF16)
-        ts[1, xt] = jnp.where(half, pltpu.roll(first, 64, 1), second).astype(BF16)
-        if d:
-            remote(ts.at[0, xt], tr.at[x * 2 + c], t_send, t_recv, x=xt, c=0)
-            remote(ts.at[1, xt], tr.at[x * 2 + c], t_send, t_recv, x=xt, c=1)
-        else:
-            remote(ts.at[other, x], tr.at[x * 2 + c], t_send, t_recv, c=other)
-            tr[x * 2 + c] = ts[c, x]
-
-    arrived(bg.at[pl.ds(0, 7)], b_recv)
-    for i in range(N):
-        block = bg[i].astype(F32)
-        sgu[i * 64 : i * 64 + 32, :] = block.astype(BF16)
-        sgu[i * 64 + 32 : i * 64 + 64, :] = pltpu.roll(block, 64, 1).astype(BF16)
-    chosen = dot(oh[x], sgu[...])
-    total = jnp.where(half, chosen[0:64], pltpu.roll(chosen[64:128], 64, 1))
-
-    arrived(tr.at[pl.ds(0, 15)], t_recv)
-    summed = tr[0].astype(F32)
-    for i in range(1, 2 * N):
-        summed = summed + tr[i].astype(F32)
-    o1[...] = (total + summed).reshape(8, 8, 128).astype(BF16)
-
-    def z_step(d, carry):
-        zt = rot(z, d)
-        remote(o1.at[zt], r1.at[z], z_send, z_recv, z=zt)
-        return carry
-
-    lax.fori_loop(1, N, z_step, 0)
-    r1[z] = o1[z]
-
-    for d in (4, 3, 5, 2, 6, 1, 7, 0):
+    here = x * N + z
+    for i in range(0, N, 2):
+        chosen = dot(oh[i : i + 2].reshape(256, ROWS), pn[...])
+        for k in range(2):
+            first, second = chosen[k * 128 : k * 128 + 64], chosen[k * 128 + 64 : k * 128 + 128]
+            to0 = jnp.where(half, first, pltpu.roll(second, 64, 1))
+            to1 = jnp.where(half, pltpu.roll(first, 64, 1), second)
+            ts[i + k] = jnp.where(c == 0, to0, to1).reshape(8, 8, 128).astype(BF16)
+            d = FAR_FIRST[i + k]
+
+            def t_step(j, carry, i=i, k=k, d=d):
+                zt = rot(z, offset_of(N - 1 - j))
+                remote(ts.at[i + k, zt], tr.at[here], t_send, t_recv, x=rot(x, d), z=zt)
+                return carry
+
+            lax.fori_loop(0, N if d else N - 1, t_step, 0)
+    tr[here] = ts[N - 1, z]
+
+    for d in FAR_FIRST:
         xt = rot(x, d)
         part = (part0[xt] + part1[:, xt]).reshape(128, 256)
         top, bottom = part[0:64], part[64:128]
@@ -357,8 +357,12 @@
             remote(cs.at[other, x], cr.at[x * 2 + c], c_send, c_recv, c=other)
             cr[x * 2 + c] = cs[c, x]
 
-    arrived(r1.at[pl.ds(0, 7)], z_recv)
-    tf[...] = r1[...].astype(F32).reshape(64, 128)
+    arrived(tr.at[pl.ds(0, 63)], t_recv)
+    for i in range(N):
+        block = tr[i].astype(F32)
+        for k in range(1, N):
+            block = block + tr[k * N + i].astype(F32)
+        tf[i * 8 : i * 8 + 8, :] = block
     for i in range(N):
         t2[i] = tf[pl.ds(i, 8, stride=8), :].astype(BF16)
 
@@ -387,9 +391,8 @@
     for i in range(4):
         arrived(g0.at[pl.ds(0, 7), pl.ds(0, 4)], ring_send.at[i])
     arrived(cr.at[pl.ds(0, 15)], c_send)
-    arrived(bg.at[pl.ds(0, 7)], b_send)
-    arrived(tr.at[pl.ds(0, 15)], t_send)
-    arrived(r1.at[pl.ds(0, 7)], z_send)
+    arrived(tr.at[pl.ds(0, 63)], t_send)
+    arrived(pin, u_send)
     arrived(r2.at[pl.ds(0, 15)], y_send)
 
 
@@ -442,17 +445,15 @@
             pltpu.VMEM((8, 8, 16, 512), BF16),
             pltpu.VMEM((8, 8, 16, 256), F32),
             pltpu.VMEM((8, 8, 16, 256), F32),
+            pltpu.VMEM((8, 8, 8, 128), F32),
+            pltpu.VMEM((8, 4, 8, 128), BF16),
+            pltpu.VMEM((8, 4, 8, 128), BF16),
             pltpu.VMEM((ROWS, 128), BF16),
+            pltpu.VMEM((8, 8, 8, 128), BF16),
+            pltpu.VMEM((64, 8, 128), BF16),
             pltpu.VMEM((2, 8, 64, 128), BF16),
             pltpu.VMEM((16, 64, 128), BF16),
-            pltpu.VMEM((2, 8, 64, 128), BF16),
-            pltpu.VMEM((16, 64, 128), BF16),
-            pltpu.VMEM((32, 128), BF16),
-            pltpu.VMEM((8, 32, 128), BF16),
-            pltpu.VMEM((ROWS, 128), BF16),
             pltpu.VMEM((8, 128, ROWS), BF16),
-            pltpu.VMEM((8, 8, 128), BF16),
-            pltpu.VMEM((8, 8, 128), BF16),
             pltpu.VMEM((64, 128), F32),
             pltpu.VMEM((8, 8, 128), BF16),
             dma((10,)),
@@ -465,10 +466,9 @@
             dma((2, 4)),
             dma((4,)),
             dma((4, 14)),
-            dma,
-            dma,
-            dma,
-            dma,
+            pltpu.SemaphoreType.REGULAR,
+            dma,
+            dma((2,)),
             dma,
             dma,
             dma,

time: 64.7 us -> 61.5 us (0.951)
  Pallas kernels: 64 us -> 60.7 us
    pallas_call x1, Pallas kernels: 63.2 us -> 59.9 us  [shards(): pl.pallas_call(kernel, out_shape=(jax.ShapeDtypeStruct((128, 128), BF16),...]
where the time goes in v3:
time: 61.5 us; the launch traced here: 61.3 us
  Pallas kernels  60.7 us (99%)
  between operations  0.64 us (1%)
    pallas_call x1, Pallas kernels, shards(): pl.pallas_call(kernel, out_shape=(jax.ShapeDtypeStruct((128, 128), BF16),...  59.9 us

profile of v3, /device:TPU:1, one launch (start us, length us, event | category | flops | bytes accessed | tf_op | source)
XLA Modules:
  0.0 61.3 jit_solution(7308091355729457451)
XLA Ops:
  0.6 59.9 %decode.1 = (bf16[128,128]{1,0:T(8,128)(2,1)S(1)}, bf16[16,8,128]{2,1,0:T(8,128)(2,1)S(1)}) custom-call(s32[4]{0:T(128)} %len_hbm.1, bf16[4,4,8,128]{3,2,1,0:T(8,128)(2,1)} %q_hbm.1, bf16[4,1536,128]{2,1,0:T(8,128)(2,1)} %bitcast.11, bf16[4,1536,128]{2,1,0:T(8,128)(2,1)} %bitcast.12, bf16[16,128]{1,0:T(8,128)(2,1)} %bitcast.14, bf16[16,128]{1,0:T(8,128)(2,1)} %bitcast.15, ...), custom_call_target="tpu_custom_call" | custom-call | tf_op jit(solution)/shard_map/decode/pallas_call | solution.py:423
  60.6 0.8 %finish.1 = (bf16[4,64,64]{2,1,0:T(8,128)(2,1)}, bf16[1,1,8192]{2,1,0:T(2,128)(2,1)}) custom-call(bf16[128,128]{1,0:T(8,128)(2,1)S(1)} %get-tuple-element.4.rows_ref, bf16[16,8,128]{2,1,0:T(8,128)(2,1)S(1)} %get-tuple-element.5.r2_ref), custom_call_target="tpu_custom_call" | custom-call | tf_op jit(solution)/shard_map/finish/pallas_call | solution.py:493
